TPU v7x, 32 devices: a whole 2x2x4 slice. The times are simulated.
32 devices in a mesh: gx: 8 (over y, x, core), gy: 4 (over z).
Axes of the slice: x: 2, y: 2, z: 4, core: 2. Of those that a mesh axis runs over, the one named last changes fastest.
Arguments:
- states: bfloat16 [512, 2048], P('gx'), may hold values from -6 to 6
- attn_gain: bfloat16 [2048], replicated, may hold values from 0.099609375 to 1.8984375
- w_qkv: bfloat16 [2048, 5120], P(None, 'gy'), may hold values from -0.125 to 0.125
- q_gain: bfloat16 [128], replicated, may hold values from 0.099609375 to 1.8984375
- k_gain: bfloat16 [128], replicated, may hold values from 0.099609375 to 1.8984375
- cache_k: bfloat16 [8, 4096, 512], P('gx', 'gy'), may hold values from -400 to 400
- cache_v: bfloat16 [8, 4096, 512], P('gx', 'gy'), may hold values from -6 to 6
- cache_len: int32 [8], P('gx'), may hold values from 256 to 4096, as said below
- tree_mask: int32 [8, 64, 64], P('gx'), may hold values from 0 to 1, as said below
- w_o: bfloat16 [4096, 2048], P(None, 'gy'), may hold values from -0.09375 to 0.09375
- ffn_gain: bfloat16 [2048], P('gy'), may hold values from 0.099609375 to 1.8984375
- routing: int32 [512, 8], replicated, may hold values from 0 to 63, all different within a row; in each aligned block of 64 rows (0 to 63, 64 to 127, ...) at most 12 rows name the same one
- route_weight: float32 [512, 8], replicated, may hold values from 0.05 to 0.5
- w_in: bfloat16 [64, 2048, 1536], P('gx', 'gy'), may hold values from -0.125 to 0.125
- w_down: bfloat16 [64, 768, 2048], P('gx', None, 'gy'), may hold values from -0.21875 to 0.21875
- accept: int32 [8, 8, 64], P('gx'), may hold values from 0 to 1, as said below
Outputs:
- layer_out: bfloat16 [512, 2048], P('gx', 'gy')
- accepted_kv: bfloat16 [8, 8, 1024], P('gx')
Inputs may be any that keep to these rules, and one draw needn't show every extreme that they name: `cache_len`: each request's cache holds keys at positions below its length; some request fills all 4096 positions. tree_mask[r, t, u] is 1 exactly when draft token u is t or an ancestor of t in request r's tree; every token's parent has a lower index and token 0 is the root. Row a of accept[r] is the one-hot of the token at depth a on one path from the root of request r's tree; the path is longer than 8 tokens. `routing`: each row names 8 different experts; in each aligned block of 64 rows no expert is named by more than 12 rows.
All inputs are finite; a program needn't handle non-finite values.
Results may differ from a plain program's by a relative error of at most 0.014.
Values may be sent and summed in bfloat16 or wider, within the bound.
A program may use at most 128 MiB of HBM per device.

v0:
```python
import math
import jax
import jax.numpy as jnp
from jax import lax
from jax.sharding import PartitionSpec as P

EPS = 1e-06
NEG = -1e30
THETA_LOG = math.log(1000000.0)


def combined_all(shard, axis, join):
    gathered = jax.tree.map(
        lambda a, kind: lax.all_gather(a.astype(kind), axis),
        shard,
        (jnp.bfloat16, jnp.bfloat16, jnp.bfloat16),
    )

    def take(source):
        return jax.tree.map(
            lambda a, own: lax.dynamic_index_in_dim(a, source, 0, False).astype(own.dtype),
            gathered,
            shard,
        )

    return lax.fori_loop(
        1, lax.axis_size(axis), lambda source, state: join(state, take(source)), take(0)
    )


def rms_scale(values, gain):
    return values * lax.rsqrt(jnp.mean(values * values, -1, keepdims=True) + EPS) * gain


def rotate(values, position):
    half = values.shape[-1] // 2
    freqs = jnp.exp(jnp.arange(half, dtype=jnp.float32) * (-2.0 * THETA_LOG / values.shape[-1]))
    angles = position.astype(jnp.float32)[..., None] * freqs
    cosine = jnp.cos(angles)
    sine = jnp.sin(angles)
    lower = values[..., :half]
    upper = values[..., half:]
    return jnp.concatenate([lower * cosine - upper * sine, upper * cosine + lower * sine], -1)


def combine_parts(earlier, later):
    max_one, sum_one, acc_one = earlier
    max_two, sum_two, acc_two = later
    joined = jnp.maximum(max_one, max_two)
    factor_one = jnp.exp(max_one - joined)
    factor_two = jnp.exp(max_two - joined)
    return (
        joined,
        sum_one * factor_one + sum_two * factor_two,
        acc_one * factor_one[..., None] + acc_two * factor_two[..., None],
    )


def body(
    states,
    attn_gain,
    w_qkv,
    q_gain,
    k_gain,
    cache_k,
    cache_v,
    cache_len,
    tree_mask,
    w_o,
    ffn_gain,
    routing,
    route_weight,
    w_in,
    w_down,
    accept,
):
    tok_rows, model_width = states.shape
    head_dim = q_gain.shape[0]
    kv_cols = cache_k.shape[2]
    kv_heads = kv_cols // head_dim
    heads_all = w_o.shape[0] // head_dim
    group = heads_all // kv_heads
    requests_here, tree_size = (tree_mask.shape[0], tree_mask.shape[1])
    cache_span = cache_k.shape[1]
    cols_here = w_o.shape[1]
    col_index = lax.axis_index("gy")
    row_index = lax.axis_index("gx")
    count_gx = lax.axis_size("gx")
    normed = rms_scale(states.astype(jnp.float32), attn_gain.astype(jnp.float32)).astype(
        jnp.bfloat16
    )
    qkv_part = jnp.dot(normed, w_qkv, preferred_element_type=jnp.float32).astype(jnp.bfloat16)
    qkv_whole = lax.all_gather(qkv_part, "gy", axis=1, tiled=True)
    q_cols = heads_all * head_dim
    query = qkv_whole[:, :q_cols].reshape(requests_here, tree_size, kv_heads, group, head_dim)
    keys_new = qkv_whole[:, q_cols : q_cols + kv_cols].reshape(
        requests_here, tree_size, kv_heads, head_dim
    )
    values_new = qkv_whole[:, q_cols + kv_cols :].reshape(
        requests_here, tree_size, kv_heads, head_dim
    )
    depth = jnp.sum(tree_mask, -1) - 1
    position = cache_len[:, None] + depth
    q_rot = rotate(
        rms_scale(query.astype(jnp.float32), q_gain.astype(jnp.float32)), position[:, :, None, None]
    ).astype(jnp.bfloat16)
    k_rot = rotate(
        rms_scale(keys_new.astype(jnp.float32), k_gain.astype(jnp.float32)), position[:, :, None]
    ).astype(jnp.bfloat16)
    cached_keys = cache_k.reshape(requests_here, cache_span, kv_heads, head_dim)
    cached_values = cache_v.reshape(requests_here, cache_span, kv_heads, head_dim)
    score_scale = head_dim ** (-0.5)
    scores_cache = (
        jnp.einsum("rtkgd,rskd->rtkgs", q_rot, cached_keys, preferred_element_type=jnp.float32)
        * score_scale
    )
    scores_tree = (
        jnp.einsum("rtkgd,rukd->rtkgu", q_rot, k_rot, preferred_element_type=jnp.float32)
        * score_scale
    )
    cache_pos = col_index * cache_span + jnp.arange(cache_span, dtype=jnp.int32)
    valid = (cache_pos[None, :] < cache_len[:, None])[:, None, None, None, :]
    tree_ok = ((tree_mask == 1) & (col_index == 0))[:, :, None, None, :]
    scores_cache = jnp.where(valid, scores_cache, NEG)
    scores_tree = jnp.where(tree_ok, scores_tree, NEG)
    row_max = jnp.maximum(jnp.max(scores_cache, -1), jnp.max(scores_tree, -1))
    probs_cache = jnp.where(valid, jnp.exp(scores_cache - row_max[..., None]), 0.0).astype(
        jnp.bfloat16
    )
    probs_tree = jnp.where(tree_ok, jnp.exp(scores_tree - row_max[..., None]), 0.0).astype(
        jnp.bfloat16
    )
    denom_sum = jnp.sum(probs_cache.astype(jnp.float32), -1) + jnp.sum(
        probs_tree.astype(jnp.float32), -1
    )
    weighted = jnp.einsum(
        "rtkgs,rskd->rtkgd", probs_cache, cached_values, preferred_element_type=jnp.float32
    )
    weighted = weighted + jnp.einsum(
        "rtkgu,rukd->rtkgd", probs_tree, values_new, preferred_element_type=jnp.float32
    )
    row_max, denom_sum, weighted = combined_all((row_max, denom_sum, weighted), "gy", combine_parts)
    attn = (weighted / denom_sum[..., None]).astype(jnp.bfloat16).reshape(tok_rows, q_cols)
    states_here = lax.dynamic_slice_in_dim(states, col_index * cols_here, cols_here, 1)
    resid = (
        states_here.astype(jnp.float32) + jnp.dot(attn, w_o, preferred_element_type=jnp.float32)
    ).astype(jnp.bfloat16)
    exp_here = w_in.shape[0]
    expert_count = exp_here * count_gx
    top_k = routing.shape[1]
    most_rows = 3 * tok_rows * top_k // (2 * expert_count)
    hidden_units = w_down.shape[1]
    gain_float = ffn_gain.astype(jnp.float32)
    own_route = lax.dynamic_slice_in_dim(routing, row_index * tok_rows, tok_rows, 0)
    own_weight = lax.dynamic_slice_in_dim(route_weight, row_index * tok_rows, tok_rows, 0)
    matched = own_route[:, :, None] == jnp.arange(expert_count, dtype=jnp.int32)[None, None, :]
    hit_count = jnp.any(matched, 1).astype(jnp.int32)
    weight_table = jnp.sum(jnp.where(matched, own_weight[:, :, None], 0.0), 1)
    slot_rank = jnp.cumsum(hit_count, 0) - 1
    slot_ids = jnp.where(
        hit_count > 0,
        jnp.arange(expert_count, dtype=jnp.int32)[None, :] * most_rows + slot_rank,
        expert_count * most_rows,
    )
    token_ids = jnp.broadcast_to(jnp.arange(tok_rows, dtype=jnp.int32)[:, None], slot_ids.shape)
    slot_table = (
        jnp.full((expert_count * most_rows,), tok_rows, jnp.int32)
        .at[slot_ids]
        .set(token_ids, mode="drop")
    )
    padded = jnp.concatenate([resid, jnp.zeros((1, cols_here), jnp.bfloat16)], 0)
    outgoing = padded[slot_table].reshape(expert_count, most_rows, cols_here)
    arrived = lax.all_to_all(outgoing, "gx", split_axis=0, concat_axis=1, tiled=True)
    arrived_float = arrived.astype(jnp.float32)
    squares = jnp.sum(arrived_float * arrived_float, -1)
    scaled = (arrived_float * gain_float).astype(jnp.bfloat16)
    partial_value = jnp.einsum("esd,edf->esf", scaled, w_in, preferred_element_type=jnp.float32)
    summed, squares = (
        lax.psum_scatter(
            partial_value.astype(jnp.bfloat16), "gy", scatter_dimension=1, tiled=True
        ).astype(jnp.float32),
        lax.psum_scatter(
            squares.astype(jnp.bfloat16), "gy", scatter_dimension=1, tiled=True
        ).astype(jnp.float32),
    )
    inverse = lax.rsqrt(squares / model_width + EPS)[..., None]
    hidden = (
        jax.nn.silu(summed[..., :hidden_units] * inverse) * (summed[..., hidden_units:] * inverse)
    ).astype(jnp.bfloat16)
    expert_out = jnp.einsum(
        "esf,efd->esd",
        lax.all_gather(hidden, "gy", axis=1, tiled=True),
        w_down,
        preferred_element_type=jnp.float32,
    )
    returned = lax.all_to_all(
        expert_out.astype(jnp.bfloat16), "gx", split_axis=1, concat_axis=0, tiled=True
    ).astype(expert_out.dtype)
    weight_pad = jnp.concatenate([weight_table, jnp.zeros((1, expert_count), jnp.float32)], 0)
    slot_expert = jnp.arange(expert_count * most_rows, dtype=jnp.int32) // most_rows
    slot_weight = weight_pad[slot_table, slot_expert]
    moe_total = (
        jnp.zeros((tok_rows + 1, cols_here), jnp.float32)
        .at[slot_table]
        .add(returned.reshape(-1, cols_here) * slot_weight[:, None])[:tok_rows]
    )
    layer_out = (resid.astype(jnp.float32) + moe_total).astype(jnp.bfloat16)
    kv_new = jnp.concatenate(
        [
            k_rot.reshape(requests_here, tree_size, kv_cols),
            values_new.reshape(requests_here, tree_size, kv_cols),
        ],
        -1,
    )
    accepted_kv = jnp.einsum(
        "rat,rtc->rac", accept.astype(jnp.bfloat16), kv_new, preferred_element_type=jnp.float32
    ).astype(jnp.bfloat16)
    return (layer_out, accepted_kv)


def solution(mesh):
    in_specs = (
        P("gx", None),
        P(),
        P(None, "gy"),
        P(),
        P(),
        P("gx", "gy", None),
        P("gx", "gy", None),
        P("gx"),
        P("gx", None, None),
        P(None, "gy"),
        P("gy"),
        P(),
        P(),
        P("gx", "gy", None),
        P("gx", None, "gy"),
        P("gx", None, None),
    )
    out_specs = (P("gx", "gy"), P("gx", None, None))
    return jax.shard_map(body, mesh=mesh, in_specs=in_specs, out_specs=out_specs, check_vma=False)
```

profile of v0, /device:TPU:0, one launch (start us, length us, event | category | flops | bytes accessed | tf_op | source)
XLA Modules:
  0.0 285.0 jit_solution(2547359270046433330)
XLA Ops:
  9.1 3.7 %convolution_convert_fusion.1 = bf16[64,1280]{1,0:T(8,128)(2,1)S(1)} fusion(bf16[2048,1280]{1,0:T(8,128)(2,1)} %param.20, bf16[64,2048]{1,0:T(8,128)(2,1)} %param.18, f32[2048]{0:T(1024)S(1)} %convert_element_type.348, f32[64]{0:T(128)S(1)} %add_rsqrt_fusion.3), kind=kOutput, calls=%fused_computation.23 | convolution fusion | flops 336150528 | bytes 5677312 | tf_op jit(solution)/shard_map/dot_general | solution.py:92
  12.7 19.6 %all_gather.20 = bf16[64,5120]{1,0:T(8,128)(2,1)S(1)} all-gather(bf16[64,1280]{1,0:T(8,128)(2,1)S(1)} %convolution_convert_fusion.1), channel_id=1, replica_groups=mesh['gx'=8,'gy'=4] {'gy'}, dimensions={1}, use_global_device_ids=true | all-gather | bytes 819200 | tf_op jit(solution)/shard_map/all_gather | solution.py:93
  36.4 4.7 %fusion.6 = (f32[64,4,8]{2,0,1:T(8,128)S(1)}, f32[4,64,8,1024]{3,2,1,0:T(8,128)}) fusion(pred[1024]{0:T(1024)(128)(4,1)S(1)} %add_compare_fusion, bf16[64,4,8,128]{3,2,0,1:T(8,128)(2,1)S(1)} %pad_maximum_fusion, bf16[1024,4,128,1]{2,1,0,3:T(4,128)(2,1)S(1)} %bitcast.184), kind=kOutput, calls=%fused_computation.18 | convolution fusion | flops 543160320 | bytes 9970688 | tf_op jit(solution)/shard_map/rtkgd,rskd->rtkgs/dot_general | solution.py:114
  43.9 5.5 %fusion.24 = bf16[1,64,4,8,128]{4,3,1,2,0:T(8,128)(2,1)S(1)} fusion(f32[4,128,64,8]{1,3,2,0:T(8,128)S(1)} %fusion.56, bf16[1024,4,128,1]{2,1,0,3:T(4,128)(2,1)S(1)} %bitcast.189, f32[4,64,8,1024]{3,2,1,0:T(8,128)} %get-tuple-element.264, f32[64,4,8]{2,0,1:T(8,128)S(1)} %copy.215, pred[1024]{0:T(1024)(128)(4,1)S(1)} %add_compare_fusion), kind=kOutput, calls=%fused_computation.38 | convolution fusion | flops 547880960 | bytes 11019264 | tf_op jit(solution)/shard_map/rtkgs,rskd->rtkgd/dot_general | solution.py:136
  51.4 15.4 %fusion.77 = s32[64,64,1]{2,1,0:T(8,128)S(1)} fusion(s32[64,64,1]{2,1,0:T(8,128)S(1)} %copy.232), kind=kOutput, calls=%fused_computation.141 | output fusion | flops 258048 | bytes 32768 | tf_op jit(solution)/shard_map/jit(cumsum)/reduce_window_sum | solution.py:159
  68.3 16.1 %all-gather = bf16[256,4,8]{2,1,0:T(4,128)(2,1)S(1)} all-gather(bf16[64,4,8]{2,1,0:T(4,128)(2,1)S(1)} %copy.214), channel_id=2, replica_groups=mesh['gx'=8,'gy'=4] {'gy'}, dimensions={0}, use_global_device_ids=true | all-gather | bytes 20480 | tf_op jit(solution)/shard_map/all_gather | solution.py:14
  84.6 4.7 %convert_reduce_fusion = f32[64,4,8]{2,0,1:T(8,128)S(1)} fusion(f32[64,4,8]{2,0,1:T(8,128)S(1)} %copy.215, f32[4,64,8,1024]{3,2,1,0:T(8,128)} %get-tuple-element.264, pred[1024]{0:T(1024)(128)(4,1)S(1)} %add_compare_fusion), kind=kLoop, calls=%fused_computation.16 | loop fusion | flops 14678016 | bytes 8406016 | tf_op jit(solution)/shard_map/reduce_sum | solution.py:133
  89.5 15.9 %all-gather.1 = bf16[256,4,8]{2,1,0:T(4,128)(2,1)S(1)} all-gather(bf16[64,4,8]{2,1,0:T(4,128)(2,1)S(1)} %copy.217), channel_id=3, replica_groups=mesh['gx'=8,'gy'=4] {'gy'}, dimensions={0}, use_global_device_ids=true | all-gather | bytes 20480 | tf_op jit(solution)/shard_map/all_gather | solution.py:14
  105.8 15.5 %scatter_custom_fusion = s32[768]{0:T(1024)S(1)} fusion(s32[4096]{0:T(1024)S(1)} %reshape.728, s32[4096]{0:T(1024)S(1)} %reshape.730, s32[]{:T(128)} %constant.123.clone.1), kind=kCustom, calls=%fused_computation.123 | custom fusion | bytes 3076 | tf_op jit(solution)/shard_map/scatter | solution.py:169
  122.5 6.7 %while.19 = (s32[]{:T(128)}, f32[1,64,4,8]{1,3,2,0:T(8,128)S(1)}, f32[1,64,4,8]{1,3,2,0:T(8,128)S(1)}, f32[1,64,4,8,128]{4,3,2,1,0:T(8,128)S(1)}, bf16[4,1,64,4,...) while((s32[]{:T(128)}, f32[1,64,4,8]{1,3,2,0:T(8,128)S(1)}, ...), condition=%wide.region_9.10_spmd, body=%wide.region_8.9_spmd.sunk | while | flops 1069061 | bytes 2764955 | solution.py:26
  122.8 1.9 fusion.92
  130.0 3.0 %fusion.27 = bf16[64,512]{1,0:T(8,128)(2,1)S(1)} fusion(bf16[64,4096]{1,0:T(8,128)(2,1)S(1)} %reshape.695, bf16[4096,512]{1,0:T(8,128)(2,1)} %param.27, bf16[64,2048]{1,0:T(8,128)(2,1)} %param.18, s32[]{:T(128)S(6)} %select_n.93), kind=kOutput, calls=%fused_computation.40 | convolution fusion | flops 268533760 | bytes 4849668 | tf_op jit(solution)/shard_map/dot_general | solution.py:146
  133.0 2.7 gather_fusion
  136.9 3.6 %all-to-all-start = ((bf16[64,12,512]{2,1,0:T(8,128)(2,1)}), bf16[64,12,512]{2,1,0:T(8,128)(2,1)S(1)}, u32[]{:S(2)}, u32[]{:S(2)}) async-start(bf16[64,12,512]{2,1,0:T(8,128)(2,1)} %reshape.696), calls=%async_computation | async-start | bytes 2097152 | tf_op jit(solution)/shard_map/all_to_all | solution.py:173
  140.6 15.3 %all-to-all-done = bf16[64,12,512]{2,1,0:T(8,128)(2,1)S(1)} async-done(((bf16[64,12,512]{2,1,0:T(8,128)(2,1)}), bf16[64,12,512]{2,1,0:T(8,128)(2,1)S(1)}, u32[]{:S(2)}, u32[]{:S(2)}) %all-to-all-start) | async-done | bytes 786464 | tf_op jit(solution)/shard_map/all_to_all | solution.py:173
  156.6 6.7 %fusion.74 = bf16[12,8,8,1536]{3,1,0,2:T(8,128)(2,1)S(1)} fusion(bf16[8,512,1536]{2,1,0:T(8,128)(2,1)} %param.31, bf16[8,96,512]{2,0,1:T(8,128)(2,1)S(1)} %fusion.10), kind=kOutput, calls=%fused_computation.140 | convolution fusion | flops 1209139200 | bytes 15728640 | tf_op jit(solution)/shard_map/esd,edf->esf/dot_general | solution.py:177
  167.6 11.3 %all-reduce.2 = bf16[8,96]{1,0:T(8,128)(2,1)S(1)} all-reduce(bf16[8,96]{1,0:T(8,128)(2,1)S(1)} %convert_element_type.390), channel_id=6, replica_groups=mesh['gx'=8,'gy'=4] {'gy'}, use_global_device_ids=true, to_apply=%region_15.16.clone | all-reduce | flops 768 | bytes 3072
  179.0 32.8 %reduce-scatter.5.cloned.1.call-done = bf16[24,12288]{1,0:T(8,128)(2,1)} async-done(((bf16[96,12288]{1,0:T(8,128)(2,1)}), bf16[24,12288]{1,0:T(8,128)(2,1)}) %reduce-scatter.5.cloned.1.call-update) | async-done | bytes 589840
  214.3 30.1 %all-gather.6.cloned.1.call-done = bf16[8,96,768]{2,1,0:T(8,128)(2,1)} async-done(((bf16[8,24,768]{2,1,0:T(8,128)(2,1)}), bf16[8,96,768]{2,1,0:T(8,128)(2,1)}) %all-gather.6.cloned.1.call-update) | async-done | bytes 1179664 | tf_op jit(solution)/shard_map/all_gather | solution.py:192
  244.4 4.3 %convolution_convert_fusion.2 = bf16[8,96,512]{2,1,0:T(8,128)(2,1)S(1)} fusion(bf16[8,96,768]{2,1,0:T(8,128)(2,1)} %all-gather.6.cloned.1.call-done, bf16[8,768,512]{2,1,0:T(8,128)(2,1)} %param.32), kind=kOutput, calls=%fused_computation.31 | convolution fusion | flops 604372992 | bytes 8257536 | tf_op jit(solution)/shard_map/esf,efd->esd/dot_general | solution.py:190
  250.0 3.8 %all-to-all-start.1 = ((bf16[8,96,512]{2,0,1:T(8,128)(2,1)}), bf16[8,96,512]{2,0,1:T(8,128)(2,1)S(1)}, u32[]{:S(2)}, u32[]{:S(2)}) async-start(bf16[8,96,512]{2,0,1:T(8,128)(2,1)} %copy.238), calls=%async_computation.1 | async-start | bytes 1572864 | tf_op jit(solution)/shard_map/all_to_all | solution.py:196
  254.9 5.1 %gather_fusion.1 = f32[768]{0:T(1024)S(1)} fusion(f32[65,64]{1,0:T(8,128)S(1)} %concatenate.45, s32[768]{0:T(1024)S(1)} %fusion.62), kind=kCustom, calls=%fused_computation.1 | custom fusion | bytes 12288 | tf_op jit(solution)/shard_map/gather | solution.py:201
  260.9 5.3 %all-to-all-done.1 = bf16[8,96,512]{2,0,1:T(8,128)(2,1)S(1)} async-done(((bf16[8,96,512]{2,0,1:T(8,128)(2,1)}), bf16[8,96,512]{2,0,1:T(8,128)(2,1)S(1)}, u32[]{:S(2)}, u32[]{:S(2)}) %all-to-all-start.1) | async-done | bytes 786464 | tf_op jit(solution)/shard_map/all_to_all | solution.py:196
  268.8 9.0 %scatter_custom_fusion.1 = f32[65,512]{1,0:T(8,128)S(1)} fusion(s32[768]{0:T(1024)S(1)} %get-tuple-element.260, f32[768,512]{1,0:T(8,128)} %reshape.709, f32[768]{0:T(1024)S(1)} %gather_fusion.1, f32[]{:T(128)} %constant.113.clone.1), kind=kCustom, calls=%fused_computation.29 | custom fusion | flops 786432 | bytes 1710084 | tf_op jit(solution)/shard_map/scatter-add | solution.py:205
  (139 shorter events, 32.8 us)
Async XLA Ops:
  7.2 43.1 %copy-start = (s32[512,8]{0,1:T(8,128)S(1)}, s32[512,8]{0,1:T(8,128)}, u32[]{:S(2)}) copy-start(s32[512,8]{0,1:T(8,128)} %param.29) | copy-start | bytes 49156
  7.2 114.2 %all-gather.8.cloned.1.call-start = ((), (), s32[]{:S(2)}) async-start(), calls=%async_computation.4 | async-start | bytes 2621440 | tf_op jit(solution)/shard_map/all_gather | solution.py:14
  12.7 21.2 %copy-start.8 = (bf16[128]{0:T(256)(128)(2,1)S(1)}, bf16[128]{0:T(256)(128)(2,1)}, u32[]{:S(2)}) copy-start(bf16[128]{0:T(256)(128)(2,1)} %param.21) | copy-start | bytes 772
  32.4 2.2 copy-start.4
  32.4 2.3 copy-start.2
  36.4 4.8 %copy-start.9 = (bf16[128]{0:T(256)(128)(2,1)S(1)}, bf16[128]{0:T(256)(128)(2,1)}, u32[]{:S(2)}) copy-start(bf16[128]{0:T(256)(128)(2,1)} %param.22) | copy-start | bytes 772
  41.8 1.4 copy-start.3
  135.7 4.8 %copy-start.6 = (bf16[512]{0:T(512)(128)(2,1)S(1)}, bf16[512]{0:T(512)(128)(2,1)}, u32[]{:S(2)}) copy-start(bf16[512]{0:T(512)(128)(2,1)} %param.28) | copy-start | bytes 3076
  136.9 19.0 %all-to-all-start = ((bf16[64,12,512]{2,1,0:T(8,128)(2,1)}), bf16[64,12,512]{2,1,0:T(8,128)(2,1)S(1)}, u32[]{:S(2)}, u32[]{:S(2)}) async-start(bf16[64,12,512]{2,1,0:T(8,128)(2,1)} %reshape.696), calls=%async_computation | async-start | bytes 2097152 | tf_op jit(solution)/shard_map/all_to_all | solution.py:173
  140.5 71.4 %reduce-scatter.5.cloned.1.call-start = ((), (), s32[]{:S(2)}) async-start(), calls=%async_computation.5 | async-start | bytes 2949120
  165.0 0.7 copy-start.10
  165.0 79.4 %all-gather.6.cloned.1.call-start = ((), (), s32[]{:S(2)}) async-start(), calls=%async_computation.3 | async-start | bytes 1474560 | tf_op jit(solution)/shard_map/all_gather | solution.py:192
  250.0 16.3 %all-to-all-start.1 = ((bf16[8,96,512]{2,0,1:T(8,128)(2,1)}), bf16[8,96,512]{2,0,1:T(8,128)(2,1)S(1)}, u32[]{:S(2)}, u32[]{:S(2)}) async-start(bf16[8,96,512]{2,0,1:T(8,128)(2,1)} %copy.238), calls=%async_computation.1 | async-start | bytes 1572864 | tf_op jit(solution)/shard_map/all_to_all | solution.py:196
  254.9 5.3 %copy-start.5 = (bf16[1,64,512]{2,1,0:T(8,128)(2,1)S(1)}, bf16[1,64,512]{2,1,0:T(8,128)(2,1)}, u32[]{:S(2)}) copy-start(bf16[1,64,512]{2,1,0:T(8,128)(2,1)} %get-tuple-element.254) | copy-start | bytes 196612
  254.9 5.3 %copy-start.7 = (s32[1,8,64]{2,1,0:T(8,128)S(1)}, s32[1,8,64]{2,1,0:T(8,128)}, u32[]{:S(2)}) copy-start(s32[1,8,64]{2,1,0:T(8,128)} %param.33) | copy-start | bytes 6148
  266.5 11.9 %copy-start.1 = (s32[512,8]{0,1:T(8,128)S(1)}, s32[512,8]{0,1:T(8,128)}, u32[]{:S(2)}) copy-start(s32[512,8]{0,1:T(8,128)} %param.29) | copy-start | bytes 49156
Sparse Core Ops, SparseCore 0:
  50.4 54.0 all-gather.7
  165.1 46.7 reduce-scatter.4
  214.4 29.9 all-gather.5
where the time goes:
time: 286 us; the launch traced here: 285 us
  waiting for transfers between devices  83.7 us (29%)
  blocking collectives  63 us (22%)
  other arithmetic  46 us (16%)
  local copies, waits for them, and re-layouts  39.4 us (14%)
  matrix products  29.6 us (10%)
  between operations  15.7 us (5%)
  starting transfers between devices  7.49 us (3%)
    unnamed x4, waiting for transfers between devices  32.9 us
    all_gather x2, blocking collectives, combined_all(): lax.all_gather(a.astype(kind), axis)  32 us
    all_gather x1, waiting for transfers between devices, body(): lax.all_gather(hidden, 'gy', axis=1, tiled=True)  30.1 us
    all_gather x1, blocking collectives, body(): qkv_whole = lax.all_gather(qkv_part, 'gy', axis=1, tiled=True)  19.6 us
    scatter x1, local copies, waits for them, and re-layouts, body(): slot_table = jnp.full((expert_count * most_rows,), tok_rows, jnp.int32).a...  15.5 us
    another operation x1, other arithmetic, body(): slot_rank = jnp.cumsum(hit_count, 0) - 1  15.4 us
    all_to_all x1, waiting for transfers between devices, body(): lax.all_to_all(outgoing, 'gx', split_axis=0, concat_axis=1, tiled=True)  15.3 us
    unnamed x1, blocking collectives  11.3 us
  transfers between devices with their start and end apart: 5, of which 4 were waited for; matrix products, arithmetic and copies ran while one was open for 17% of the time, Pallas kernels for 0%

commit v1 on v0

--- a/solution.py
+++ b/solution.py
@@ -7,6 +7,19 @@
 EPS = 1e-06
 NEG = -1e30
 THETA_LOG = math.log(1000000.0)
+
+
+def gather_around(array, axis, dim):
+    ways = lax.axis_size(axis)
+    up = [(d, (d + 1) % ways) for d in range(ways)]
+    down = [(d, (d - 1) % ways) for d in range(ways)]
+    earlier, later = ([array], [array])
+    for _ in range(ways // 2):
+        earlier.append(lax.ppermute(earlier[-1], axis, up))
+    for _ in range((ways - 1) // 2):
+        later.append(lax.ppermute(later[-1], axis, down))
+    line = jnp.concatenate([*earlier[::-1], *later[1:]], axis=dim)
+    return jnp.roll(line, (lax.axis_index(axis) - ways // 2) * array.shape[dim], axis=dim)
 
 
 def combined_all(shard, axis, join):
@@ -188,10 +201,7 @@
         jax.nn.silu(summed[..., :hidden_units] * inverse) * (summed[..., hidden_units:] * inverse)
     ).astype(jnp.bfloat16)
     expert_out = jnp.einsum(
-        "esf,efd->esd",
-        lax.all_gather(hidden, "gy", axis=1, tiled=True),
-        w_down,
-        preferred_element_type=jnp.float32,
+        "esf,efd->esd", gather_around(hidden, "gy", 1), w_down, preferred_element_type=jnp.float32
     )
     returned = lax.all_to_all(
         expert_out.astype(jnp.bfloat16), "gx", split_axis=1, concat_axis=0, tiled=True

time: 286 us -> 280 us (0.979)
  waiting for transfers between devices: 83.7 us -> 73.5 us
  starting transfers between devices: 7.49 us -> 11.6 us
    all_gather x1 -> x0, waiting for transfers between devices: 30.1 us -> none  [body(): lax.all_gather(hidden, 'gy', axis=1, tiled=True)]
    ppermute x0 -> x3, waiting for transfers between devices: none -> 19.9 us  [the longest x2 17.8 us: gather_around(): earlier.append(lax.ppermute(earlier[-1], axis, up))]
    ppermute x0 -> x3, starting transfers between devices: none -> 4.42 us  [the longest x1 3.82 us: gather_around(): later.append(lax.ppermute(later[-1], axis, down))]
    unnamed x4 -> x3, waiting for transfers between devices: 32.9 us -> 32.9 us
  transfers between devices with their start and end apart: 5 -> 7, of which waited for: 4 -> 6; matrix products, arithmetic and copies ran while one was open for 17% -> 17% of each run, Pallas kernels for 0% -> 0%
where the time goes in v1:
time: 280 us; the launch traced here: 279 us
  waiting for transfers between devices  73.5 us (26%)
  blocking collectives  63 us (22%)
  other arithmetic  45.7 us (16%)
  local copies, waits for them, and re-layouts  39.5 us (14%)
  matrix products  29.2 us (10%)
  between operations  16.1 us (6%)
  starting transfers between devices  11.6 us (4%)
    unnamed x3, waiting for transfers between devices  32.9 us
    all_gather x2, blocking collectives, combined_all(): lax.all_gather(a.astype(kind), axis)  32 us
    all_gather x1, blocking collectives, body(): qkv_whole = lax.all_gather(qkv_part, 'gy', axis=1, tiled=True)  19.6 us
    ppermute x2, waiting for transfers between devices, gather_around(): earlier.append(lax.ppermute(earlier[-1], axis, up))  17.8 us
    scatter x1, local copies, waits for them, and re-layouts, body(): slot_table = jnp.full((expert_count * most_rows,), tok_rows, jnp.int32).a...  15.5 us
    another operation x1, other arithmetic, body(): slot_rank = jnp.cumsum(hit_count, 0) - 1  15.4 us
    all_to_all x1, waiting for transfers between devices, body(): lax.all_to_all(outgoing, 'gx', split_axis=0, concat_axis=1, tiled=True)  15.3 us
    unnamed x1, blocking collectives  11.3 us
  transfers between devices with their start and end apart: 7, of which 6 were waited for; matrix products, arithmetic and copies ran while one was open for 17% of the time, Pallas kernels for 0%

profile of v1, /device:TPU:0, one launch (start us, length us, event | category | flops | bytes accessed | tf_op | source)
XLA Modules:
  0.0 278.9 jit_solution(16132391632648228486)
XLA Ops:
  9.1 3.7 %convolution_convert_fusion.1 = bf16[64,1280]{1,0:T(8,128)(2,1)S(1)} fusion(bf16[2048,1280]{1,0:T(8,128)(2,1)} %param.20, bf16[64,2048]{1,0:T(8,128)(2,1)} %param.18, f32[2048]{0:T(1024)S(1)} %convert_element_type.348, f32[64]{0:T(128)S(1)} %add_rsqrt_fusion.3), kind=kOutput, calls=%fused_computation.23 | convolution fusion | flops 336150528 | bytes 5677312 | tf_op jit(solution)/shard_map/dot_general | solution.py:105
  12.7 19.6 %all_gather.17 = bf16[64,5120]{1,0:T(8,128)(2,1)S(1)} all-gather(bf16[64,1280]{1,0:T(8,128)(2,1)S(1)} %convolution_convert_fusion.1), channel_id=1, replica_groups=mesh['gx'=8,'gy'=4] {'gy'}, dimensions={1}, use_global_device_ids=true | all-gather | bytes 819200 | tf_op jit(solution)/shard_map/all_gather | solution.py:106
  36.4 4.7 %fusion.6 = (f32[64,4,8]{2,0,1:T(8,128)S(1)}, f32[4,64,8,1024]{3,2,1,0:T(8,128)}) fusion(pred[1024]{0:T(1024)(128)(4,1)S(1)} %add_compare_fusion, bf16[64,4,8,128]{3,2,0,1:T(8,128)(2,1)S(1)} %pad_maximum_fusion, bf16[1024,4,128,1]{2,1,0,3:T(4,128)(2,1)S(1)} %bitcast.183), kind=kOutput, calls=%fused_computation.18 | convolution fusion | flops 543160320 | bytes 9970688 | tf_op jit(solution)/shard_map/rtkgd,rskd->rtkgs/dot_general | solution.py:127
  43.9 5.5 %fusion.24 = bf16[1,64,4,8,128]{4,3,1,2,0:T(8,128)(2,1)S(1)} fusion(f32[4,128,64,8]{1,3,2,0:T(8,128)S(1)} %fusion.57, bf16[1024,4,128,1]{2,1,0,3:T(4,128)(2,1)S(1)} %bitcast.188, f32[4,64,8,1024]{3,2,1,0:T(8,128)} %get-tuple-element.264, f32[64,4,8]{2,0,1:T(8,128)S(1)} %copy.215, pred[1024]{0:T(1024)(128)(4,1)S(1)} %add_compare_fusion), kind=kOutput, calls=%fused_computation.38 | convolution fusion | flops 547880960 | bytes 11019264 | tf_op jit(solution)/shard_map/rtkgs,rskd->rtkgd/dot_general | solution.py:149
  51.4 15.4 %fusion.79 = s32[64,64,1]{2,1,0:T(8,128)S(1)} fusion(s32[64,64,1]{2,1,0:T(8,128)S(1)} %copy.232), kind=kOutput, calls=%fused_computation.151 | output fusion | flops 258048 | bytes 32768 | tf_op jit(solution)/shard_map/jit(cumsum)/reduce_window_sum | solution.py:172
  68.3 16.1 %all-gather = bf16[256,4,8]{2,1,0:T(4,128)(2,1)S(1)} all-gather(bf16[64,4,8]{2,1,0:T(4,128)(2,1)S(1)} %copy.214), channel_id=2, replica_groups=mesh['gx'=8,'gy'=4] {'gy'}, dimensions={0}, use_global_device_ids=true | all-gather | bytes 20480 | tf_op jit(solution)/shard_map/all_gather | solution.py:27
  84.6 4.7 %convert_reduce_fusion = f32[64,4,8]{2,0,1:T(8,128)S(1)} fusion(f32[64,4,8]{2,0,1:T(8,128)S(1)} %copy.215, f32[4,64,8,1024]{3,2,1,0:T(8,128)} %get-tuple-element.264, pred[1024]{0:T(1024)(128)(4,1)S(1)} %add_compare_fusion), kind=kLoop, calls=%fused_computation.16 | loop fusion | flops 14678016 | bytes 8406016 | tf_op jit(solution)/shard_map/reduce_sum | solution.py:146
  89.5 15.9 %all-gather.1 = bf16[256,4,8]{2,1,0:T(4,128)(2,1)S(1)} all-gather(bf16[64,4,8]{2,1,0:T(4,128)(2,1)S(1)} %copy.217), channel_id=3, replica_groups=mesh['gx'=8,'gy'=4] {'gy'}, dimensions={0}, use_global_device_ids=true | all-gather | bytes 20480 | tf_op jit(solution)/shard_map/all_gather | solution.py:27
  105.8 15.5 %scatter_custom_fusion = s32[768]{0:T(1024)S(1)} fusion(s32[4096]{0:T(1024)S(1)} %reshape.728, s32[4096]{0:T(1024)S(1)} %reshape.730, s32[]{:T(128)} %constant.142.clone.1), kind=kCustom, calls=%fused_computation.132 | custom fusion | bytes 3076 | tf_op jit(solution)/shard_map/scatter | solution.py:182
  122.5 6.7 %while.19 = (s32[]{:T(128)}, f32[1,64,4,8]{1,3,2,0:T(8,128)S(1)}, f32[1,64,4,8]{1,3,2,0:T(8,128)S(1)}, f32[1,64,4,8,128]{4,3,2,1,0:T(8,128)S(1)}, bf16[4,1,64,4,...) while((s32[]{:T(128)}, f32[1,64,4,8]{1,3,2,0:T(8,128)S(1)}, ...), condition=%wide.region_9.10_spmd, body=%wide.region_8.9_spmd.sunk | while | flops 1069061 | bytes 2764955 | solution.py:39
  130.0 3.0 %fusion.28 = bf16[64,512]{1,0:T(8,128)(2,1)S(1)} fusion(bf16[64,4096]{1,0:T(8,128)(2,1)S(1)} %reshape.695, bf16[4096,512]{1,0:T(8,128)(2,1)} %param.27, bf16[64,2048]{1,0:T(8,128)(2,1)} %param.18, s32[]{:T(128)S(6)} %select_n.106), kind=kOutput, calls=%fused_computation.41 | convolution fusion | flops 268533760 | bytes 4849668 | tf_op jit(solution)/shard_map/dot_general | solution.py:159
  136.9 3.6 %all-to-all-start = ((bf16[64,12,512]{2,1,0:T(8,128)(2,1)}), bf16[64,12,512]{2,1,0:T(8,128)(2,1)S(1)}, u32[]{:S(2)}, u32[]{:S(2)}) async-start(bf16[64,12,512]{2,1,0:T(8,128)(2,1)} %reshape.696), calls=%async_computation | async-start | bytes 2097152 | tf_op jit(solution)/shard_map/all_to_all | solution.py:186
  140.6 15.3 %all-to-all-done = bf16[64,12,512]{2,1,0:T(8,128)(2,1)S(1)} async-done(((bf16[64,12,512]{2,1,0:T(8,128)(2,1)}), bf16[64,12,512]{2,1,0:T(8,128)(2,1)S(1)}, u32[]{:S(2)}, u32[]{:S(2)}) %all-to-all-start) | async-done | bytes 786464 | tf_op jit(solution)/shard_map/all_to_all | solution.py:186
  156.6 6.7 %fusion.76 = bf16[12,8,8,1536]{3,1,0,2:T(8,128)(2,1)S(1)} fusion(bf16[8,512,1536]{2,1,0:T(8,128)(2,1)} %param.31, bf16[8,96,512]{2,0,1:T(8,128)(2,1)S(1)} %fusion.10), kind=kOutput, calls=%fused_computation.150 | convolution fusion | flops 1209139200 | bytes 15728640 | tf_op jit(solution)/shard_map/esd,edf->esf/dot_general | solution.py:190
  167.6 11.3 %all-reduce.2 = bf16[8,96]{1,0:T(8,128)(2,1)S(1)} all-reduce(bf16[8,96]{1,0:T(8,128)(2,1)S(1)} %convert_element_type.390), channel_id=6, replica_groups=mesh['gx'=8,'gy'=4] {'gy'}, use_global_device_ids=true, to_apply=%region_15.16.clone | all-reduce | flops 768 | bytes 3072
  179.0 32.8 %reduce-scatter.5.cloned.1.call-done = bf16[24,12288]{1,0:T(8,128)(2,1)} async-done(((bf16[96,12288]{1,0:T(8,128)(2,1)}), bf16[24,12288]{1,0:T(8,128)(2,1)}) %reduce-scatter.5.cloned.1.call-update) | async-done | bytes 589840
  214.2 9.9 %collective-permute-done = bf16[8,24,768]{2,1,0:T(8,128)(2,1)S(1)} collective-permute-done((bf16[8,24,768]{2,1,0:T(8,128)(2,1)S(1)}, bf16[8,24,768]{2,1,0:T(8,128)(2,1)S(1)}, u32[]{:S(2)}, u32[]{:S(2)}) %collective-permute-start) | collective-permute-done | bytes 294944 | tf_op jit(solution)/shard_map/ppermute | solution.py:18
  224.1 3.8 %collective-permute-start.2 = (bf16[8,24,768]{2,1,0:T(8,128)(2,1)S(1)}, bf16[8,24,768]{2,1,0:T(8,128)(2,1)S(1)}, u32[]{:S(2)}, u32[]{:S(2)}) collective-permute-start(bf16[8,24,768]{2,1,0:T(8,128)(2,1)S(1)} %fusion.37), channel_id=1, source_target_pairs={{0,3},{1,0},{2,1},{3,2},{4,7},{5,4},{6,5},{7,6},{8,11},{9,8},{10,9... | collective-permute-start | bytes 884744 | tf_op jit(solution)/shard_map/ppermute | solution.py:20
  227.9 7.9 %collective-permute-done.1 = bf16[8,24,768]{2,1,0:T(8,128)(2,1)S(1)} collective-permute-done((bf16[8,24,768]{2,1,0:T(8,128)(2,1)S(1)}, bf16[8,24,768]{2,1,0:T(8,128)(2,1)S(1)}, u32[]{:S(2)}, u32[]{:S(2)}) %collective-permute-start.1) | collective-permute-done | bytes 294944 | tf_op jit(solution)/shard_map/ppermute | solution.py:18
  238.5 4.0 %convolution_convert_fusion.2 = bf16[8,96,512]{2,1,0:T(8,128)(2,1)S(1)} fusion(bf16[8,768,512]{2,1,0:T(8,128)(2,1)} %param.32, bf16[8,192,768]{2,1,0:T(8,128)(2,1)S(1)} %constant_dynamic-update-slice_fusion, s32[]{:T(128)S(6)} %select_n.117), kind=kOutput, calls=%fused_computation.31 | convolution fusion | flops 604372992 | bytes 8257540 | tf_op jit(solution)/shard_map/esf,efd->esd/dot_general | solution.py:203
  243.8 3.5 %all-to-all-start.1 = ((bf16[8,96,512]{2,0,1:T(8,128)(2,1)}), bf16[8,96,512]{2,0,1:T(8,128)(2,1)S(1)}, u32[]{:S(2)}, u32[]{:S(2)}) async-start(bf16[8,96,512]{2,0,1:T(8,128)(2,1)} %copy.238), calls=%async_computation.1 | async-start | bytes 1572864 | tf_op jit(solution)/shard_map/all_to_all | solution.py:206
  248.5 5.1 %gather_fusion.1 = f32[768]{0:T(1024)S(1)} fusion(f32[65,64]{1,0:T(8,128)S(1)} %concatenate.52, s32[768]{0:T(1024)S(1)} %fusion.63), kind=kCustom, calls=%fused_computation.1 | custom fusion | bytes 12288 | tf_op jit(solution)/shard_map/gather | solution.py:211
  254.5 5.4 %all-to-all-done.1 = bf16[8,96,512]{2,0,1:T(8,128)(2,1)S(1)} async-done(((bf16[8,96,512]{2,0,1:T(8,128)(2,1)}), bf16[8,96,512]{2,0,1:T(8,128)(2,1)S(1)}, u32[]{:S(2)}, u32[]{:S(2)}) %all-to-all-start.1) | async-done | bytes 786464 | tf_op jit(solution)/shard_map/all_to_all | solution.py:206
  262.4 9.0 %scatter_custom_fusion.1 = f32[65,512]{1,0:T(8,128)S(1)} fusion(s32[768]{0:T(1024)S(1)} %get-tuple-element.260, f32[768,512]{1,0:T(8,128)} %reshape.709, f32[768]{0:T(1024)S(1)} %gather_fusion.1, f32[]{:T(128)} %constant.132.clone.1), kind=kCustom, calls=%fused_computation.29 | custom fusion | flops 786432 | bytes 1710084 | tf_op jit(solution)/shard_map/scatter-add | solution.py:215
  (150 shorter events, 40.0 us)
Async XLA Ops:
  7.2 43.1 %copy-start = (s32[512,8]{0,1:T(8,128)S(1)}, s32[512,8]{0,1:T(8,128)}, u32[]{:S(2)}) copy-start(s32[512,8]{0,1:T(8,128)} %param.29) | copy-start | bytes 49156
  7.2 114.2 %all-gather.5.cloned.1.call-start = ((), (), s32[]{:S(2)}) async-start(), calls=%async_computation.3 | async-start | bytes 2621440 | tf_op jit(solution)/shard_map/all_gather | solution.py:27
  12.7 21.2 %copy-start.8 = (bf16[128]{0:T(256)(128)(2,1)S(1)}, bf16[128]{0:T(256)(128)(2,1)}, u32[]{:S(2)}) copy-start(bf16[128]{0:T(256)(128)(2,1)} %param.21) | copy-start | bytes 772
  32.4 2.2 copy-start.4
  32.4 2.3 copy-start.2
  36.4 4.8 %copy-start.9 = (bf16[128]{0:T(256)(128)(2,1)S(1)}, bf16[128]{0:T(256)(128)(2,1)}, u32[]{:S(2)}) copy-start(bf16[128]{0:T(256)(128)(2,1)} %param.22) | copy-start | bytes 772
  41.8 1.4 copy-start.3
  135.7 4.8 %copy-start.6 = (bf16[512]{0:T(512)(128)(2,1)S(1)}, bf16[512]{0:T(512)(128)(2,1)}, u32[]{:S(2)}) copy-start(bf16[512]{0:T(512)(128)(2,1)} %param.28) | copy-start | bytes 3076
  136.9 19.0 %all-to-all-start = ((bf16[64,12,512]{2,1,0:T(8,128)(2,1)}), bf16[64,12,512]{2,1,0:T(8,128)(2,1)S(1)}, u32[]{:S(2)}, u32[]{:S(2)}) async-start(bf16[64,12,512]{2,1,0:T(8,128)(2,1)} %reshape.696), calls=%async_computation | async-start | bytes 2097152 | tf_op jit(solution)/shard_map/all_to_all | solution.py:186
  140.5 71.4 %reduce-scatter.5.cloned.1.call-start = ((), (), s32[]{:S(2)}) async-start(), calls=%async_computation.4 | async-start | bytes 2949120
  165.0 0.7 copy-start.10
  213.6 10.5 %collective-permute-start = (bf16[8,24,768]{2,1,0:T(8,128)(2,1)S(1)}, bf16[8,24,768]{2,1,0:T(8,128)(2,1)S(1)}, u32[]{:S(2)}, u32[]{:S(2)}) collective-permute-start(bf16[8,24,768]{2,1,0:T(8,128)(2,1)S(1)} %fusion.37), channel_id=1, source_target_pairs={{0,1},{1,2},{2,3},{3,0},{4,5},{5,6},{6,7},{7,4},{8,9},{9,10},{10,1... | collective-permute-start | bytes 884744 | tf_op jit(solution)/shard_map/ppermute | solution.py:18
  224.1 11.7 %collective-permute-start.1 = (bf16[8,24,768]{2,1,0:T(8,128)(2,1)S(1)}, bf16[8,24,768]{2,1,0:T(8,128)(2,1)S(1)}, u32[]{:S(2)}, u32[]{:S(2)}) collective-permute-start(bf16[8,24,768]{2,1,0:T(8,128)(2,1)S(1)} %collective-permute-done), channel_id=1, source_target_pairs={{0,1},{1,2},{2,3},{3,0},{4,5},{5,6},{6,7},{7,4},{8,9},{9,10},{10,1... | collective-permute-start | bytes 884744 | tf_op jit(solution)/shard_map/ppermute | solution.py:18
  224.1 14.1 %collective-permute-start.2 = (bf16[8,24,768]{2,1,0:T(8,128)(2,1)S(1)}, bf16[8,24,768]{2,1,0:T(8,128)(2,1)S(1)}, u32[]{:S(2)}, u32[]{:S(2)}) collective-permute-start(bf16[8,24,768]{2,1,0:T(8,128)(2,1)S(1)} %fusion.37), channel_id=1, source_target_pairs={{0,3},{1,0},{2,1},{3,2},{4,7},{5,4},{6,5},{7,6},{8,11},{9,8},{10,9... | collective-permute-start | bytes 884744 | tf_op jit(solution)/shard_map/ppermute | solution.py:20
  243.8 16.1 %all-to-all-start.1 = ((bf16[8,96,512]{2,0,1:T(8,128)(2,1)}), bf16[8,96,512]{2,0,1:T(8,128)(2,1)S(1)}, u32[]{:S(2)}, u32[]{:S(2)}) async-start(bf16[8,96,512]{2,0,1:T(8,128)(2,1)} %copy.238), calls=%async_computation.1 | async-start | bytes 1572864 | tf_op jit(solution)/shard_map/all_to_all | solution.py:206
  248.5 5.3 %copy-start.5 = (bf16[1,64,512]{2,1,0:T(8,128)(2,1)S(1)}, bf16[1,64,512]{2,1,0:T(8,128)(2,1)}, u32[]{:S(2)}) copy-start(bf16[1,64,512]{2,1,0:T(8,128)(2,1)} %get-tuple-element.254) | copy-start | bytes 196612
  248.5 5.3 %copy-start.7 = (s32[1,8,64]{2,1,0:T(8,128)S(1)}, s32[1,8,64]{2,1,0:T(8,128)}, u32[]{:S(2)}) copy-start(s32[1,8,64]{2,1,0:T(8,128)} %param.33) | copy-start | bytes 6148
  260.1 11.9 %copy-start.1 = (s32[512,8]{0,1:T(8,128)S(1)}, s32[512,8]{0,1:T(8,128)}, u32[]{:S(2)}) copy-start(s32[512,8]{0,1:T(8,128)} %param.29) | copy-start | bytes 49156
Sparse Core Ops, SparseCore 0:
  50.4 54.0 all-gather.4
  165.1 46.7 reduce-scatter.4
